TPU v7x, 32 devices: a whole 2x2x4 slice. The times are simulated.
32 devices in a mesh: dp: 16 (over z, y, x), tensor: 2 (over core).
Axes of the slice: x: 2, y: 2, z: 4, core: 2. Of those that a mesh axis runs over, the one named last changes fastest.
Arguments:
- tokens: bfloat16 [24576, 768], P(('dp', 'tensor')), may hold values from -6 to 6
- kept_patches: int32 [24576], P(('dp', 'tensor')), may hold values from 0 to 1567, as said below
- clip_lengths: int32 [128], replicated, may hold values from 39 to 314, as said below
- clip_device: int32 [128], replicated, may hold values from 0 to 31, as said below
- cot_output: bfloat16 [24576, 768], P(('dp', 'tensor')), may hold values from -6 to 6
- cot_aligned: bfloat16 [24576, 1024], P(('dp', 'tensor')), may hold values from -6 to 6
- entry_weight: float32 [1769472], P(('dp', 'tensor')), may hold values from -0.21875 to 0.21875
- entry_first: float32 [1769472], P(('dp', 'tensor')), may hold values from -112 to 112
- entry_second: float32 [1769472], P(('dp', 'tensor')), may hold values from 245.76 to 4096.8193
- exit_weight: float32 [589824], P(('dp', 'tensor')), may hold values from -1.75 to 1.75
- exit_first: float32 [589824], P(('dp', 'tensor')), may hold values from -24 to 24
- exit_second: float32 [589824], P(('dp', 'tensor')), may hold values from 12.288 to 204.71808
- align_weight: float32 [786432], P(('dp', 'tensor')), may hold values from -0.21875 to 0.21875
- align_first: float32 [786432], P(('dp', 'tensor')), may hold values from -128 to 128
- align_second: float32 [786432], P(('dp', 'tensor')), may hold values from 447.2832 to 8183.808
- expand_weight: float32 [3072, 768], P(('dp', 'tensor')), may hold values from -0.21875 to 0.21875
- expand_first: float32 [3072, 768], P(('dp', 'tensor')), may hold values from -32 to 32
- expand_second: float32 [3072, 768], P(('dp', 'tensor')), may hold values from 24.576 to 409.68192
- reduce_weight: float32 [3072, 768], P(('dp', 'tensor')), may hold values from -0.109375 to 0.109375
- reduce_first: float32 [3072, 768], P(('dp', 'tensor')), may hold values from -80 to 80
- reduce_second: float32 [3072, 768], P(('dp', 'tensor')), may hold values from 144.50688 to 2457.6
- position_table: float32 [1204224], P(('dp', 'tensor')), may hold values from -3 to 3
- position_first: float32 [1204224], P(('dp', 'tensor')), may hold values from -5 to 5
- position_second: float32 [1204224], P(('dp', 'tensor')), may hold values from 0.5219265 to 7.836735
- norm_params: float32 [3072], P(('dp', 'tensor')), may hold values from -1.5 to 1.5, as said below
- norm_first: float32 [3072], P(('dp', 'tensor')), may hold values from -128 to 128
- norm_second: float32 [3072], P(('dp', 'tensor')), may hold values from 447.2832 to 8183.808
Outputs:
- block_out: bfloat16 [24576, 768], P(('dp', 'tensor'))
- aligned: bfloat16 [24576, 1024], P(('dp', 'tensor'))
- token_grad: float32 [24576, 768], P(('dp', 'tensor'))
- new_entry_first: float32 [1769472], P(('dp', 'tensor'))
- new_entry_second: float32 [1769472], P(('dp', 'tensor'))
- new_entry_weight: float32 [1769472], P(('dp', 'tensor'))
- new_exit_first: float32 [589824], P(('dp', 'tensor'))
- new_exit_second: float32 [589824], P(('dp', 'tensor'))
- new_exit_weight: float32 [589824], P(('dp', 'tensor'))
- new_align_first: float32 [786432], P(('dp', 'tensor'))
- new_align_second: float32 [786432], P(('dp', 'tensor'))
- new_align_weight: float32 [786432], P(('dp', 'tensor'))
- new_expand_first: float32 [3072, 768], P(('dp', 'tensor'))
- new_expand_second: float32 [3072, 768], P(('dp', 'tensor'))
- new_expand_weight: float32 [3072, 768], P(('dp', 'tensor'))
- new_reduce_first: float32 [3072, 768], P(('dp', 'tensor'))
- new_reduce_second: float32 [3072, 768], P(('dp', 'tensor'))
- new_reduce_weight: float32 [3072, 768], P(('dp', 'tensor'))
- new_position_first: float32 [1204224], P(('dp', 'tensor'))
- new_position_second: float32 [1204224], P(('dp', 'tensor'))
- new_position_table: float32 [1204224], P(('dp', 'tensor'))
- new_norm_first: float32 [3072], P(('dp', 'tensor'))
- new_norm_second: float32 [3072], P(('dp', 'tensor'))
- new_norm_params: float32 [3072], P(('dp', 'tensor'))
- lamb_stats: float32 [3, 7], replicated
Inputs may be any that keep to these rules, and one draw needn't show every extreme that they name: `clip_lengths`: every clip has 314 rows (a video clip) or 39 rows (an image). `clip_device`: each device index d = i * 2 + j holds exactly 4 clips, at most 2 of them video clips, and some device holds 2. `kept_patches`: within a video clip the rows hold distinct positions below 1568 in rising order, within an image distinct positions below 196 in rising order; padding rows hold 0. `norm_params`: gains lie in 0.5 to 1.5; shifts are normal of deviation 0.5, held within -1.5 to 1.5.
All inputs are finite; a program needn't handle non-finite values.
Results may differ from a plain program's by a relative error of at most 0.0085.
The roundings to bfloat16 on the way count: a program that leaves them out, or rounds other values in their place, can miss the bound.
Values may be sent and summed in bfloat16 or wider, within the bound.
A program may use at most 192 MiB of HBM per device.

v0:
```python
import jax
import jax.numpy as jnp
from jax import lax
from jax.sharding import PartitionSpec as P

H = 12
HD = 64
LN_EPS = 1e-06
MASKED = -1e30
RATE = 0.5
BETA_ONE = 0.9
BETA_TWO = 0.98
ADAM_EPS = 1e-06
DECAY = 0.05
TINY = 1e-06


def contract(left, right, left_dim, right_dim):
    return lax.dot_general(
        left, right, (((left_dim,), (right_dim,)), ((), ())), preferred_element_type=jnp.float32
    )


def layer_norm(values, gain, shift):
    center = values - jnp.mean(values, axis=-1, keepdims=True)
    spread = jnp.mean(center * center, axis=-1, keepdims=True)
    return center * lax.rsqrt(spread + LN_EPS) * gain + shift


def gelu_exact(values):
    return jax.nn.gelu(values, approximate=False)


def row_layout(clip_lengths, clip_device, device, row_count):
    mine = clip_device == device
    own_length = jnp.where(mine, clip_lengths, 0)
    starts = jnp.cumsum(own_length) - own_length
    filled = jnp.sum(own_length)
    positions = jnp.arange(row_count, dtype=jnp.int32)
    begun = mine[None, :] & (starts[None, :] <= positions[:, None])
    segment = jnp.sum(begun.astype(jnp.int32), axis=1)
    valid_rows = positions < filled
    return (jnp.where(valid_rows, segment, 0), valid_rows)


def head_scores(queries, key_rows, same_clip, score_scale):
    scores = contract(queries, key_rows, 1, 1) * score_scale
    return jnp.where(same_clip, scores, MASKED)


def head_forward(queries, key_rows, value_rows, same_clip, score_scale):
    scores = head_scores(queries, key_rows, same_clip, score_scale)
    peak_score = jnp.max(scores, axis=1, keepdims=True)
    raised = jnp.exp(scores - peak_score)
    row_total = jnp.sum(raised, axis=1, keepdims=True)
    attention = raised / row_total
    result = jnp.dot(attention.astype(jnp.bfloat16), value_rows, preferred_element_type=jnp.float32)
    return (result, (peak_score + jnp.log(row_total))[:, 0])


def head_backward(queries, key_rows, value_rows, log_total, grad_heads, same_clip, score_scale):
    scores = head_scores(queries, key_rows, same_clip, score_scale)
    attention = jnp.exp(scores - log_total[:, None])
    attention_low = attention.astype(jnp.bfloat16)
    grad_values = contract(attention_low, grad_heads, 0, 0)
    grad_attention = contract(grad_heads, value_rows, 1, 1)
    inner = jnp.sum(attention * grad_attention, axis=1, keepdims=True)
    grad_score = (attention * (grad_attention - inner)).astype(jnp.bfloat16)
    grad_queries = jnp.dot(grad_score, key_rows, preferred_element_type=jnp.float32) * score_scale
    grad_keys = contract(grad_score, queries, 0, 0) * score_scale
    return (grad_queries, grad_keys, grad_values)


def lamb_moments(weight, gradient, first, second, decay):
    new_first = BETA_ONE * first + (1.0 - BETA_ONE) * gradient
    new_second = BETA_TWO * second + (1.0 - BETA_TWO) * gradient * gradient
    update = new_first / (jnp.sqrt(new_second) + ADAM_EPS) + decay * weight
    return (new_first, new_second, update)


def local(
    tokens,
    kept_patches,
    clip_lengths,
    clip_device,
    cot_output,
    cot_aligned,
    entry_weight,
    entry_first,
    entry_second,
    exit_weight,
    exit_first,
    exit_second,
    align_weight,
    align_first,
    align_second,
    expand_weight,
    expand_first,
    expand_second,
    reduce_weight,
    reduce_first,
    reduce_second,
    position_table,
    position_first,
    position_second,
    norm_params,
    norm_first,
    norm_second,
):
    row_count, model_width = tokens.shape
    align_width = cot_aligned.shape[1]
    score_scale = HD ** (-0.5)
    masters = (
        entry_weight,
        exit_weight,
        align_weight,
        expand_weight,
        reduce_weight,
        position_table,
        norm_params,
    )
    device = lax.axis_index("dp") * lax.axis_size("tensor") + lax.axis_index("tensor")
    segment, valid_rows = row_layout(clip_lengths, clip_device, device, row_count)
    same_clip = segment[:, None] == segment[None, :]
    valid_column = valid_rows[:, None]
    gathered = (
        lax.all_gather(entry_weight.astype(jnp.bfloat16), ("dp", "tensor"), axis=0, tiled=True),
        lax.all_gather(exit_weight.astype(jnp.bfloat16), ("dp", "tensor"), axis=0, tiled=True),
        lax.all_gather(align_weight.astype(jnp.bfloat16), ("dp", "tensor"), axis=0, tiled=True),
        lax.all_gather(position_table.astype(jnp.bfloat16), ("dp", "tensor"), axis=0, tiled=True),
        lax.all_gather(norm_params.astype(jnp.bfloat16), ("dp", "tensor"), axis=0, tiled=True),
    )
    expand_low, reduce_low = (
        lax.all_gather(expand_weight.astype(jnp.bfloat16), "dp", axis=0, tiled=True),
        lax.all_gather(reduce_weight.astype(jnp.bfloat16), "dp", axis=0, tiled=True),
    )
    entry_low = gathered[0].reshape(model_width, 3 * model_width)
    exit_low = gathered[1].reshape(model_width, model_width)
    align_low = gathered[2].reshape(model_width, align_width)
    table_low = gathered[3].reshape(-1, model_width)
    norm_low = gathered[4].astype(jnp.float32).reshape(4, model_width)
    residual = tokens.astype(jnp.float32) + jnp.take(table_low, kept_patches, axis=0).astype(
        jnp.float32
    )
    normed_one = layer_norm(residual, norm_low[0], norm_low[1]).astype(jnp.bfloat16)
    joint_low = jnp.dot(normed_one, entry_low, preferred_element_type=jnp.float32).astype(
        jnp.bfloat16
    )
    split_heads = joint_low.reshape(row_count, 3, H, HD).transpose(1, 2, 0, 3)
    head_outputs, log_totals = lax.map(
        lambda entries: head_forward(entries[0], entries[1], entries[2], same_clip, score_scale),
        (split_heads[0], split_heads[1], split_heads[2]),
    )
    attended = head_outputs.transpose(1, 0, 2).reshape(row_count, model_width).astype(jnp.bfloat16)
    middle = residual + jnp.dot(attended, exit_low, preferred_element_type=jnp.float32)
    normed_two = layer_norm(middle, norm_low[2], norm_low[3]).astype(jnp.bfloat16)
    hidden_in = lax.all_gather(normed_two, "tensor", axis=0, tiled=True)
    hidden_pre = contract(hidden_in, expand_low, 1, 1)
    hidden_act = gelu_exact(hidden_pre).astype(jnp.bfloat16)
    feed_out = lax.psum_scatter(
        jnp.dot(hidden_act, reduce_low, preferred_element_type=jnp.float32).astype(jnp.bfloat16),
        "tensor",
        scatter_dimension=0,
        tiled=True,
    ).astype(jnp.float32)
    out_low = (middle + feed_out).astype(jnp.bfloat16)
    block_out = jnp.where(valid_column, out_low, jnp.zeros_like(out_low))
    align_rows = jnp.dot(out_low, align_low, preferred_element_type=jnp.float32).astype(
        jnp.bfloat16
    )
    aligned = jnp.where(valid_column, align_rows, jnp.zeros_like(align_rows))
    cot_align_valid = jnp.where(valid_column, cot_aligned, jnp.zeros_like(cot_aligned))
    grad_align = contract(out_low, cot_align_valid, 0, 0)
    grad_out = jnp.where(valid_column, cot_output.astype(jnp.float32), 0.0) + contract(
        cot_align_valid, align_low, 1, 1
    )
    grad_feed = grad_out.astype(jnp.bfloat16)
    grad_feed_rows = lax.all_gather(grad_feed, "tensor", axis=0, tiled=True)
    grad_act = contract(grad_feed_rows, reduce_low, 1, 1)
    gelu_value, gelu_back = jax.vjp(gelu_exact, hidden_pre)
    grad_pre = gelu_back(grad_act)[0].astype(jnp.bfloat16)
    grad_reduce = contract(hidden_act, grad_feed_rows, 0, 0)
    grad_expand = contract(grad_pre, hidden_in, 0, 0)
    grad_two = lax.psum_scatter(
        jnp.dot(grad_pre, expand_low, preferred_element_type=jnp.float32),
        "tensor",
        scatter_dimension=0,
        tiled=True,
    )
    grad_expand, grad_reduce = (
        lax.psum_scatter(grad_expand, "dp", scatter_dimension=0, tiled=True),
        lax.psum_scatter(grad_reduce, "dp", scatter_dimension=0, tiled=True),
    )
    norm_value, norm_back_two = jax.vjp(layer_norm, middle, norm_low[2], norm_low[3])
    grad_from_two, grad_gain_two, grad_shift_two = norm_back_two(grad_two)
    grad_middle = grad_out + grad_from_two
    grad_branch = grad_middle.astype(jnp.bfloat16)
    grad_exit = contract(attended, grad_branch, 0, 0)
    grad_attended = contract(grad_branch, exit_low, 1, 1).astype(jnp.bfloat16)
    grad_heads = grad_attended.reshape(row_count, H, HD).transpose(1, 0, 2)
    grad_queries, grad_keys, grad_values = lax.map(
        lambda entries: head_backward(
            entries[0], entries[1], entries[2], entries[3], entries[4], same_clip, score_scale
        ),
        (split_heads[0], split_heads[1], split_heads[2], log_totals, grad_heads),
    )
    grad_joint = jnp.stack((grad_queries, grad_keys, grad_values)).transpose(2, 0, 1, 3)
    grad_joint = grad_joint.reshape(row_count, 3 * model_width).astype(jnp.bfloat16)
    grad_entry = contract(normed_one, grad_joint, 0, 0)
    grad_one = contract(grad_joint, entry_low, 1, 1)
    norm_value_one, norm_back_one = jax.vjp(layer_norm, residual, norm_low[0], norm_low[1])
    grad_from_one, grad_gain_one, grad_shift_one = norm_back_one(grad_one)
    token_grad = grad_middle + grad_from_one
    grad_table = jax.ops.segment_sum(token_grad, kept_patches, num_segments=table_low.shape[0])
    grad_norms = jnp.concatenate((grad_gain_one, grad_shift_one, grad_gain_two, grad_shift_two))
    summed = (
        lax.psum_scatter(grad_entry.reshape(-1), ("dp", "tensor"), scatter_dimension=0, tiled=True),
        lax.psum_scatter(grad_exit.reshape(-1), ("dp", "tensor"), scatter_dimension=0, tiled=True),
        lax.psum_scatter(grad_align.reshape(-1), ("dp", "tensor"), scatter_dimension=0, tiled=True),
        lax.psum_scatter(grad_table.reshape(-1), ("dp", "tensor"), scatter_dimension=0, tiled=True),
        lax.psum_scatter(grad_norms, ("dp", "tensor"), scatter_dimension=0, tiled=True),
    )
    gradients = (summed[0], summed[1], summed[2], grad_expand, grad_reduce, summed[3], summed[4])
    firsts = (
        entry_first,
        exit_first,
        align_first,
        expand_first,
        reduce_first,
        position_first,
        norm_first,
    )
    seconds = (
        entry_second,
        exit_second,
        align_second,
        expand_second,
        reduce_second,
        position_second,
        norm_second,
    )
    decays = (DECAY, DECAY, DECAY, DECAY, DECAY, DECAY, 0.0)
    results = [
        lamb_moments(
            masters[member], gradients[member], firsts[member], seconds[member], decays[member]
        )
        for member in range(7)
    ]
    update_local = jnp.stack([jnp.sum(found[2] * found[2]) for found in results])
    weight_squares, update_squares = lax.psum(
        (jnp.stack([jnp.sum(master * master) for master in masters]), update_local),
        ("dp", "tensor"),
    )
    trust = jnp.sqrt(weight_squares) / jnp.sqrt(update_squares + TINY)
    outputs = [block_out, aligned, token_grad]
    for member in range(7):
        found = results[member]
        outputs = outputs + [found[0], found[1], masters[member] - RATE * trust[member] * found[2]]
    lamb_stats = jnp.stack((trust, jnp.sqrt(weight_squares), jnp.sqrt(update_squares)))
    outputs = outputs + [lamb_stats]
    return tuple(outputs)


def solution(mesh):
    placed = (
        P(("dp", "tensor"), None),
        P(("dp", "tensor")),
        P(),
        P(),
        P(("dp", "tensor"), None),
        P(("dp", "tensor"), None),
        P(("dp", "tensor")),
        P(("dp", "tensor")),
        P(("dp", "tensor")),
        P(("dp", "tensor")),
        P(("dp", "tensor")),
        P(("dp", "tensor")),
        P(("dp", "tensor")),
        P(("dp", "tensor")),
        P(("dp", "tensor")),
        P(("dp", "tensor"), None),
        P(("dp", "tensor"), None),
        P(("dp", "tensor"), None),
        P(("dp", "tensor"), None),
        P(("dp", "tensor"), None),
        P(("dp", "tensor"), None),
        P(("dp", "tensor")),
        P(("dp", "tensor")),
        P(("dp", "tensor")),
        P(("dp", "tensor")),
        P(("dp", "tensor")),
        P(("dp", "tensor")),
    )
    return jax.shard_map(
        local,
        mesh=mesh,
        in_specs=placed,
        out_specs=(
            P(("dp", "tensor"), None),
            P(("dp", "tensor"), None),
            P(("dp", "tensor"), None),
            P(("dp", "tensor")),
            P(("dp", "tensor")),
            P(("dp", "tensor")),
            P(("dp", "tensor")),
            P(("dp", "tensor")),
            P(("dp", "tensor")),
            P(("dp", "tensor")),
            P(("dp", "tensor")),
            P(("dp", "tensor")),
            P(("dp", "tensor"), None),
            P(("dp", "tensor"), None),
            P(("dp", "tensor"), None),
            P(("dp", "tensor"), None),
            P(("dp", "tensor"), None),
            P(("dp", "tensor"), None),
            P(("dp", "tensor")),
            P(("dp", "tensor")),
            P(("dp", "tensor")),
            P(("dp", "tensor")),
            P(("dp", "tensor")),
            P(("dp", "tensor")),
            P(),
        ),
        check_vma=False,
    )
```

profile of v0, /device:TPU:0, one launch (start us, length us, event | category | flops | bytes accessed | tf_op | source)
XLA Modules:
  0.0 1165.3 jit_solution(5532540820435427545)
XLA Ops:
  19.3 42.3 %all-reduce = bf16[3072]{0:T(1024)(128)(2,1)S(1)} all-reduce(bf16[3072]{0:T(1024)(128)(2,1)S(1)} %dynamic-update-slice), channel_id=1, replica_groups=mesh['dp'=16,'tensor'=2] {'dp','tensor'}, use_global_device_ids=true, to_apply=%add | all-reduce | flops 3072 | bytes 12288
  71.7 63.2 %all-gather.24.cloned.1.call-done = bf16[32,1,37632]{2,1,0:T(2,128)(2,1)} async-done(((bf16[1,1,37632]{2,1,0:T(2,128)(2,1)}), bf16[32,1,37632]{2,1,0:T(2,128)(2,1)}) %all-gather.24.cloned.1.call-update) | async-done | bytes 2408464 | tf_op jit(solution)/shard_map/all_gather | solution.py:130
  135.0 51.2 %reduce.1 = bf16[32,37632]{1,0:T(8,128)(2,1)} reduce(bf16[32,1,37632]{2,1,0:T(2,128)(2,1)} %all-gather.24.cloned.1.call-done, bf16[]{:T(256)} %constant.226), dimensions={1}, to_apply=%all-gather.reduce_sub_computation | reduce | bytes 4816898 | tf_op jit(solution)/shard_map/all_gather | solution.py:130
  197.4 7.6 reshape.245
  205.0 7.2 convolution_convert_fusion
  212.2 5.8 copy.127
  230.9 64.8 %while.28 = (s32[]{:T(128)}, bf16[12,768,64]{1,2,0:T(8,128)(2,1)}, f32[12,768]{1,0:T(8,128)}, bf16[12,768,64]{2,1,0:T(8,128)(2,1)}, bf16[12,768,64]{2,1,0:T(8,12...) while((s32[]{:T(128)}, bf16[12,768,64]{1,2,0:T(8,128)(2,1)}, ...), condition=%wide.region_8.9_spmd.clone, body=%wide.region_5.8_spmd.clone.sunk | while | flops 156302592 | bytes 7911521 | solution.py:150
  318.9 11.2 all-gather.14.cloned.1.call-done
  330.1 27.0 %multiply_convert_fusion.1 = (bf16[1536,1536]{1,0:T(8,128)(2,1)}, f32[1536,1536]{1,0:T(8,128)}, f32[1536,1536]{1,0:T(8,128)}) fusion(bf16[1536,768]{0,1:T(8,128)(2,1)} %all-gather.14.cloned.1.call-done, bf16[1536,768]{1,0:T(8,128)(2,1)} %all-gather.16.cloned.1.call-done), kind=kOutput, calls=%fused_computation.57 | convolution fusion | flops 3777232896 | bytes 28311552 | tf_op jit(solution)/shard_map/dot_general | solution.py:19
  357.1 9.2 fusion.95
  366.4 138.8 %reduce-scatter.11.cloned.1.call-done = f32[96,768]{1,0:T(8,128)} async-done(((f32[1536,768]{1,0:T(8,128)}), f32[96,768]{1,0:T(8,128)}) %reduce-scatter.11.cloned.1.call-update) | async-done | bytes 294928 | tf_op jit(solution)/shard_map/reduce_scatter | solution.py:192
  508.0 62.5 %all-gather.18.cloned.1.call-done = bf16[1536,768]{1,0:T(8,128)(2,1)} async-done(((bf16[96,768]{1,0:T(8,128)(2,1)}), bf16[1536,768]{1,0:T(8,128)(2,1)}) %all-gather.18.cloned.1.call-update) | async-done | bytes 2359312 | tf_op jit(solution)/shard_map/all_gather | solution.py:135
  570.5 8.5 convolution_convert_fusion.1
  579.0 14.0 %add_convert_fusion = bf16[1536,1536]{1,0:T(8,128)(2,1)S(1)} fusion(f32[1536,1536]{1,0:T(8,128)} %get-tuple-element.433, bf16[1536,768]{0,1:T(8,128)(2,1)} %all-gather.22.cloned.1.call-done, bf16[1536,768]{1,0:T(8,128)(2,1)} %all-gather.18.cloned.1.call-done, f32[1536,1536]{1,0:T(8,128)} %get-tuple-element.462), kind=kOutput, calls=%fused_computation.56 | convolution fusion | flops 3656908800 | bytes 28311552 | tf_op jit(solution)/shard_map/dot_general | solution.py:19
  595.2 5.7 fusion.92
  601.5 9.4 fusion.94
  629.6 107.8 %while.29 = (s32[]{:T(128)}, bf16[12,768,64]{1,2,0:T(8,128)(2,1)S(1)}, bf16[12,768,64]{1,2,0:T(8,128)(2,1)}, bf16[12,768,64]{1,2,0:T(8,128)(2,1)}, bf16[12,768,6...) while((s32[]{:T(128)}, ...), condition=%wide.region_17.18_spmd.clone, body=%wide.region_15.17_spmd.clone.sunk | while | flops 383483136 | bytes 19690608 | solution.py:201
  751.2 7.9 reshape.252
  759.1 7.4 fusion.91
  779.4 9.9 scatter_custom_fusion
  789.3 5.9 reshape.255
  799.7 41.4 %all-reduce.5 = f32[3072]{0:T(1024)S(1)} all-reduce(f32[3072]{0:T(1024)S(1)} %pad_maximum_fusion), channel_id=10, replica_groups=mesh['dp'=16,'tensor'=2] {'dp','tensor'}, use_global_device_ids=true, to_apply=%region_45.46.clone | all-reduce | flops 3072 | bytes 24576
  844.6 239.9 %all-reduce.10.cloned.1.call-done = (f32[1769472]{0:T(1024)}, f32[589824]{0:T(1024)}, f32[786432]{0:T(1024)}, f32[1204224]{0:T(1024)}) async-done(((f32[1769472]{0:T(1024)}, f32[589824]{0:T(1024)}, f32[786432]{0:T(1024)}, f32[1204224]{0:T(1024)}), (f32[1769472]{0:T(1024)}, f32[589824]{0:T(1024)}, f32[786432]{0:T(1024)}, f32[1204224]{0:T(1024)})) %all-reduce.10.cloned.1.call-update) | async-done | bytes 17399824
  1104.7 39.6 %all-reduce.6 = (f32[7]{0:T(128)S(1)}, f32[7]{0:T(128)S(1)}) all-reduce(f32[7]{0:T(128)S(1)} %stack.91, f32[7]{0:T(128)S(1)} %stack.83), channel_id=1, replica_groups=mesh['dp'=16,'tensor'=2] {'dp','tensor'}, use_global_device_ids=true, to_apply=%region_47.48 | all-reduce | flops 14 | bytes 112 | tf_op jit(solution)/shard_map/psum | solution.py:250
  (420 shorter events, 329.9 us)
Async XLA Ops:
  7.2 61.2 %all-gather.12.cloned.1.call-start = ((), (), s32[]{:S(2)}) async-start(), calls=%async_computation.5 | async-start | bytes 1216512 | tf_op jit(solution)/shard_map/all_gather | solution.py:128
  8.9 126.1 %all-gather.24.cloned.1.call-start = ((), (), s32[]{:S(2)}) async-start(), calls=%async_computation.15 | async-start | bytes 4967424 | tf_op jit(solution)/shard_map/all_gather | solution.py:130
  10.6 186.7 %all-gather.10.cloned.1.call-start = ((), (), s32[]{:S(2)}) async-start(), calls=%async_computation.4 | async-start | bytes 3649536 | tf_op jit(solution)/shard_map/all_gather | solution.py:127
  12.3 292.2 %all-gather.20.cloned.1.call-start = ((), (), s32[]{:S(2)}) async-start(), calls=%async_computation.10 | async-start | bytes 1622016 | tf_op jit(solution)/shard_map/all_gather | solution.py:129
  13.9 305.0 %all-gather.16.cloned.1.call-start = ((), (), s32[]{:S(2)}) async-start(), calls=%async_computation.7 | async-start | bytes 2506752 | tf_op jit(solution)/shard_map/all_gather | solution.py:134
  15.6 314.5 %all-gather.14.cloned.1.call-start = ((), (), s32[]{:S(2)}) async-start(), calls=%async_computation.6 | async-start | bytes 3538944 | tf_op jit(solution)/shard_map/all_gather | solution.py:157
  301.3 55.8 %all-gather.22.cloned.1.call-start = ((), (), s32[]{:S(2)}) async-start(), calls=%async_computation.11 | async-start | bytes 3538944 | tf_op jit(solution)/shard_map/all_gather | solution.py:178
  313.4 191.8 %reduce-scatter.11.cloned.1.call-start = ((), (), s32[]{:S(2)}) async-start(), calls=%async_computation.14 | async-start | bytes 5013504 | tf_op jit(solution)/shard_map/reduce_scatter | solution.py:192
  366.4 204.1 %all-gather.18.cloned.1.call-start = ((), (), s32[]{:S(2)}) async-start(), calls=%async_computation.8 | async-start | bytes 2506752 | tf_op jit(solution)/shard_map/all_gather | solution.py:135
  507.8 103.2 %reduce-scatter.5.cloned.1.call-start = ((), (), s32[]{:S(2)}) async-start(), calls=%async_computation.9 | async-start | bytes 3538944 | tf_op jit(solution)/shard_map/reduce_scatter | solution.py:160
  579.0 39.3 %reduce-scatter.7.cloned.1.call-start = ((), (), s32[]{:S(2)}) async-start(), calls=%async_computation.12 | async-start | bytes 7077888 | tf_op jit(solution)/shard_map/reduce_scatter | solution.py:184
  601.0 241.4 %reduce-scatter.9.cloned.1.call-start = ((), (), s32[]{:S(2)}) async-start(), calls=%async_computation.13 | async-start | bytes 5013504 | tf_op jit(solution)/shard_map/reduce_scatter | solution.py:191
  610.9 473.7 %all-reduce.10.cloned.1.call-start = ((), (), s32[]{:S(2)}) async-start(), calls=%async_computation.16 | async-start | bytes 34799616
  799.6 287.6 %copy-start.16 = (f32[37632]{0:T(1024)S(1)}, f32[37632]{0:T(1024)}, u32[]{:S(2)}) copy-start(f32[37632]{0:T(1024)} %param.52) | copy-start | bytes 451588
  799.6 287.6 %copy-start.34 = (f32[37632]{0:T(1024)S(1)}, f32[37632]{0:T(1024)}, u32[]{:S(2)}) copy-start(f32[37632]{0:T(1024)} %param.54) | copy-start | bytes 451588
  799.6 287.6 %copy-start.35 = (f32[37632]{0:T(1024)S(1)}, f32[37632]{0:T(1024)}, u32[]{:S(2)}) copy-start(f32[37632]{0:T(1024)} %param.53) | copy-start | bytes 451588
  799.6 290.1 %copy-start.30 = (f32[24576]{0:T(1024)S(1)}, f32[24576]{0:T(1024)}, u32[]{:S(2)}) copy-start(f32[24576]{0:T(1024)} %param.43) | copy-start | bytes 294916
  799.6 290.1 %copy-start.38 = (f32[24576]{0:T(1024)S(1)}, f32[24576]{0:T(1024)}, u32[]{:S(2)}) copy-start(f32[24576]{0:T(1024)} %param.45) | copy-start | bytes 294916
  799.6 290.1 %copy-start.39 = (f32[24576]{0:T(1024)S(1)}, f32[24576]{0:T(1024)}, u32[]{:S(2)}) copy-start(f32[24576]{0:T(1024)} %param.44) | copy-start | bytes 294916
  799.6 292.3 %copy-start.31 = (f32[18432]{0:T(1024)S(1)}, f32[18432]{0:T(1024)}, u32[]{:S(2)}) copy-start(f32[18432]{0:T(1024)} %param.40) | copy-start | bytes 221188
  799.7 292.3 %copy-start.40 = (f32[18432]{0:T(1024)S(1)}, f32[18432]{0:T(1024)}, u32[]{:S(2)}) copy-start(f32[18432]{0:T(1024)} %param.42) | copy-start | bytes 221188
  799.7 292.3 %copy-start.41 = (f32[18432]{0:T(1024)S(1)}, f32[18432]{0:T(1024)}, u32[]{:S(2)}) copy-start(f32[18432]{0:T(1024)} %param.41) | copy-start | bytes 221188
  844.6 312.8 %copy-start.28 = (f32[96,768]{1,0:T(8,128)}, f32[96,768]{1,0:T(8,128)S(1)}, u32[]{:S(2)}) copy-start(f32[96,768]{1,0:T(8,128)S(1)} %get-tuple-element.420) | copy-start | bytes 884740
  844.6 312.8 %copy-start.29 = (f32[96,768]{1,0:T(8,128)}, f32[96,768]{1,0:T(8,128)S(1)}, u32[]{:S(2)}) copy-start(f32[96,768]{1,0:T(8,128)S(1)} %get-tuple-element.421) | copy-start | bytes 884740
  (59 other events, 2078.1 us)
Sparse Core Ops, SparseCore 0:
  11.6 56.8 all-gather.11
  71.8 63.1 all-gather.23
  138.4 58.8 all-gather.9
  200.6 53.7 all-gather.19
  257.7 61.1 all-gather.15
  320.3 9.7 all-gather.13
  331.6 12.1 all-gather.21
  366.5 138.6 reduce-scatter.10
  508.9 61.4 all-gather.17
  579.1 8.7 reduce-scatter.4
  601.1 11.3 reduce-scatter.6
  618.4 138.7 reduce-scatter.8
  795.4 289.1 all-reduce.9
where the time goes:
time: 1180 us; the launch traced here: 1170 us
  waiting for transfers between devices  526 us (45%)
  matrix products  248 us (21%)
  other arithmetic  125 us (11%)
  blocking collectives  123 us (10%)
  local copies, waits for them, and re-layouts  122 us (10%)
  between operations  19.4 us (2%)
    unnamed x14, waiting for transfers between devices  240 us
    dot_general x70, matrix products, contract(): lax.dot_general(left, right, (((left_dim,), (right_dim,)), ((), ())), pre...  180 us
    reduce_scatter x1, waiting for transfers between devices, local(): lax.psum_scatter(grad_reduce, 'dp', scatter_dimension=0, tiled=True)  139 us
    unnamed x2, blocking collectives  83.7 us
    all_gather x1, waiting for transfers between devices, local(): lax.all_gather(position_table.astype(jnp.bfloat16), ('dp', 'tensor'), axi...  63.2 us
    all_gather x1, waiting for transfers between devices, local(): lax.all_gather(reduce_weight.astype(jnp.bfloat16), 'dp', axis=0, tiled=True)  62.5 us
    all_gather x1, other arithmetic, local(): lax.all_gather(position_table.astype(jnp.bfloat16), ('dp', 'tensor'), axi...  51.2 us
    psum x1, blocking collectives, local(): lax.psum((jnp.stack([jnp.sum(master * master) for master in masters]), up...  39.6 us
  transfers between devices with their start and end apart: 13, of which 7 were waited for; matrix products, arithmetic and copies ran while one was open for 37% of the time, Pallas kernels for 0%

commit v1 on v0

--- a/solution.py
+++ b/solution.py
@@ -1,3 +1,4 @@
+import functools
 import jax
 import jax.numpy as jnp
 from jax import lax
@@ -13,6 +14,37 @@
 ADAM_EPS = 1e-06
 DECAY = 0.05
 TINY = 1e-06
+
+
+def refer_plate(local_x, pos_dim):
+    local_x = jnp.moveaxis(local_x, 0, pos_dim)
+    extra = local_x.shape
+    return local_x.reshape(
+        *extra[:pos_dim], extra[pos_dim] * extra[pos_dim + 1], *extra[pos_dim + 2 :]
+    )
+
+
+def tell_the_sections(raw, shard_axis):
+    b_now = jax.lax.axis_size(shard_axis)
+    tile_out = jax.lax.axis_index(shard_axis)
+    outer, block_next = (b_now, tile_out)
+    plain, passed = (raw[None], 1)
+    while passed < outer:
+        z_new = jax.lax.ppermute(plain, shard_axis, [(j0, j0 ^ passed) for j0 in range(outer)])
+        spare = block_next & passed == 0
+        v1 = jnp.where(spare, plain, z_new)
+        parts_out = jnp.where(spare, z_new, plain)
+        plain = jnp.concatenate([v1, parts_out])
+        passed *= 2
+    return plain
+
+
+def pairs_all_try_all(point, panel, ndim_at):
+    out_arr = tell_the_sections(point, panel)
+    return refer_plate(out_arr, ndim_at)
+
+
+track_row = functools.partial(pairs_all_try_all, panel=("dp", "tensor"), ndim_at=0)
 
 
 def contract(left, right, left_dim, right_dim):
@@ -127,7 +159,7 @@
         lax.all_gather(entry_weight.astype(jnp.bfloat16), ("dp", "tensor"), axis=0, tiled=True),
         lax.all_gather(exit_weight.astype(jnp.bfloat16), ("dp", "tensor"), axis=0, tiled=True),
         lax.all_gather(align_weight.astype(jnp.bfloat16), ("dp", "tensor"), axis=0, tiled=True),
-        lax.all_gather(position_table.astype(jnp.bfloat16), ("dp", "tensor"), axis=0, tiled=True),
+        track_row(position_table.astype(jnp.bfloat16)),
         lax.all_gather(norm_params.astype(jnp.bfloat16), ("dp", "tensor"), axis=0, tiled=True),
     )
     expand_low, reduce_low = (

time: 1180 us -> 1130 us (0.958)
  other arithmetic: 125 us -> 77 us
  waiting for transfers between devices: 526 us -> 488 us
  blocking collectives: 123 us -> 156 us
    all_gather x1 -> x0, waiting for transfers between devices: 63.2 us -> none  [local(): lax.all_gather(position_table.astype(jnp.bfloat16), ('dp', 'tensor'), axi...]
    all_gather x1 -> x0, other arithmetic: 51.2 us -> none  [local(): lax.all_gather(position_table.astype(jnp.bfloat16), ('dp', 'tensor'), axi...]
    unnamed x2, blocking collectives: 83.7 us -> 116 us
    ppermute x0 -> x5, waiting for transfers between devices: none -> 23.1 us  [tell_the_sections(): jax.lax.ppermute(plain, shard_axis, [(j0, j0 ^ passed) for j0 in range(ou...]
    unnamed x151 -> x152, local copies, waits for them, and re-layouts: 29.1 us -> 28.9 us
    unnamed x14 -> x13, waiting for transfers between devices: 240 us -> 240 us
  transfers between devices with their start and end apart: 13 -> 17, of which waited for: 7 -> 9; matrix products, arithmetic and copies ran while one was open for 37% -> 34% of each run, Pallas kernels for 0% -> 0%
where the time goes in v1:
time: 1130 us; the launch traced here: 1120 us
  waiting for transfers between devices  488 us (43%)
  matrix products  247 us (22%)
  blocking collectives  156 us (14%)
  local copies, waits for them, and re-layouts  122 us (11%)
  other arithmetic  77 us (7%)
  between operations  19.8 us (2%)
    unnamed x13, waiting for transfers between devices  240 us
    dot_general x70, matrix products, contract(): lax.dot_general(left, right, (((left_dim,), (right_dim,)), ((), ())), pre...  179 us
    reduce_scatter x1, waiting for transfers between devices, local(): lax.psum_scatter(grad_reduce, 'dp', scatter_dimension=0, tiled=True)  139 us
    unnamed x2, blocking collectives  116 us
    all_gather x1, waiting for transfers between devices, local(): lax.all_gather(reduce_weight.astype(jnp.bfloat16), 'dp', axis=0, tiled=True)  62.6 us
    psum x1, blocking collectives, local(): lax.psum((jnp.stack([jnp.sum(master * master) for master in masters]), up...  39.6 us
    unnamed x152, local copies, waits for them, and re-layouts  28.9 us
    dot_general x12, matrix products, head_forward(): jnp.dot(attention.astype(jnp.bfloat16), value_rows, preferred_element_typ...  25.3 us
  transfers between devices with their start and end apart: 17, of which 9 were waited for; matrix products, arithmetic and copies ran while one was open for 34% of the time, Pallas kernels for 0%

profile of v1, /device:TPU:0, one launch (start us, length us, event | category | flops | bytes accessed | tf_op | source)
XLA Modules:
  0.0 1120.9 jit_solution(12619148393765771249)
XLA Ops:
  23.3 6.7 collective-permute-done.2
  33.1 13.4 %collective-permute-done.3 = bf16[8,37632]{1,0:T(8,128)(2,1)S(1)} collective-permute-done((bf16[8,37632]{1,0:T(8,128)(2,1)S(1)}, bf16[8,37632]{1,0:T(8,128)(2,1)S(1)}, u32[]{:S(2)}, u32[]{:S(2)}) %collective-permute-start.3) | collective-permute-done | bytes 602144 | tf_op jit(solution)/shard_map/ppermute | solution.py:33
  54.2 74.4 %all-reduce = bf16[3072]{0:T(1024)(128)(2,1)S(1)} all-reduce(bf16[3072]{0:T(1024)(128)(2,1)S(1)} %dynamic-update-slice), channel_id=1, replica_groups=mesh['dp'=16,'tensor'=2] {'dp','tensor'}, use_global_device_ids=true, to_apply=%add | all-reduce | flops 3072 | bytes 12288
  146.7 6.2 all-gather.8.cloned.1.call-done
  152.9 7.6 reshape.241
  160.5 6.7 convolution_convert_fusion
  185.9 64.9 %while.28 = (s32[]{:T(128)}, bf16[12,768,64]{1,2,0:T(8,128)(2,1)}, f32[12,768]{1,0:T(8,128)}, bf16[12,768,64]{2,1,0:T(8,128)(2,1)}, bf16[12,768,64]{2,1,0:T(8,12...) while((s32[]{:T(128)}, bf16[12,768,64]{1,2,0:T(8,128)(2,1)}, ...), condition=%wide.region_8.9_spmd.clone, body=%wide.region_5.8_spmd.clone.sunk | while | flops 156302592 | bytes 7911521 | solution.py:182
  268.3 6.3 all-gather.14.cloned.1.call-done
  274.5 11.2 all-gather.12.cloned.1.call-done
  285.7 26.9 %multiply_convert_fusion.1 = (bf16[1536,1536]{1,0:T(8,128)(2,1)}, f32[1536,1536]{1,0:T(8,128)}, f32[1536,1536]{1,0:T(8,128)}) fusion(bf16[1536,768]{0,1:T(8,128)(2,1)} %all-gather.12.cloned.1.call-done, bf16[1536,768]{1,0:T(8,128)(2,1)} %all-gather.14.cloned.1.call-done), kind=kOutput, calls=%fused_computation.57 | convolution fusion | flops 3777232896 | bytes 28311552 | tf_op jit(solution)/shard_map/dot_general | solution.py:51
  312.6 9.2 fusion.95
  322.1 138.6 %reduce-scatter.11.cloned.1.call-done = f32[96,768]{1,0:T(8,128)} async-done(((f32[1536,768]{1,0:T(8,128)}), f32[96,768]{1,0:T(8,128)}) %reduce-scatter.11.cloned.1.call-update) | async-done | bytes 294928 | tf_op jit(solution)/shard_map/reduce_scatter | solution.py:224
  463.3 62.6 %all-gather.16.cloned.1.call-done = bf16[1536,768]{1,0:T(8,128)(2,1)} async-done(((bf16[96,768]{1,0:T(8,128)(2,1)}), bf16[1536,768]{1,0:T(8,128)(2,1)}) %all-gather.16.cloned.1.call-update) | async-done | bytes 2359312 | tf_op jit(solution)/shard_map/all_gather | solution.py:167
  526.0 8.5 convolution_convert_fusion.1
  534.5 14.0 %add_convert_fusion = bf16[1536,1536]{1,0:T(8,128)(2,1)S(1)} fusion(f32[1536,1536]{1,0:T(8,128)} %get-tuple-element.391, bf16[1536,768]{0,1:T(8,128)(2,1)} %all-gather.20.cloned.1.call-done, bf16[1536,768]{1,0:T(8,128)(2,1)} %all-gather.16.cloned.1.call-done, f32[1536,1536]{1,0:T(8,128)} %get-tuple-element.430), kind=kOutput, calls=%fused_computation.56 | convolution fusion | flops 3656908800 | bytes 28311552 | tf_op jit(solution)/shard_map/dot_general | solution.py:51
  556.9 9.4 fusion.94
  585.0 107.6 %while.29 = (s32[]{:T(128)}, bf16[12,768,64]{1,2,0:T(8,128)(2,1)S(1)}, bf16[12,768,64]{1,2,0:T(8,128)(2,1)}, bf16[12,768,64]{1,2,0:T(8,128)(2,1)}, bf16[12,768,6...) while((s32[]{:T(128)}, ...), condition=%wide.region_17.18_spmd.clone, body=%wide.region_15.17_spmd.clone.sunk | while | flops 383483136 | bytes 19690608 | solution.py:233
  706.2 8.0 reshape.248
  714.2 7.4 fusion.91
  734.5 9.9 scatter_custom_fusion
  744.3 5.9 reshape.251
  754.7 41.7 %all-reduce.5 = f32[3072]{0:T(1024)S(1)} all-reduce(f32[3072]{0:T(1024)S(1)} %pad_maximum_fusion.5), channel_id=10, replica_groups=mesh['dp'=16,'tensor'=2] {'dp','tensor'}, use_global_device_ids=true, to_apply=%region_45.46.clone | all-reduce | flops 3072 | bytes 24576
  799.9 239.8 %all-reduce.10.cloned.1.call-done = (f32[1769472]{0:T(1024)}, f32[589824]{0:T(1024)}, f32[786432]{0:T(1024)}, f32[1204224]{0:T(1024)}) async-done(((f32[1769472]{0:T(1024)}, f32[589824]{0:T(1024)}, f32[786432]{0:T(1024)}, f32[1204224]{0:T(1024)}), (f32[1769472]{0:T(1024)}, f32[589824]{0:T(1024)}, f32[786432]{0:T(1024)}, f32[1204224]{0:T(1024)})) %all-reduce.10.cloned.1.call-update) | async-done | bytes 17399824
  1060.1 39.6 %all-reduce.6 = (f32[7]{0:T(128)S(1)}, f32[7]{0:T(128)S(1)}) all-reduce(f32[7]{0:T(128)S(1)} %stack.91, f32[7]{0:T(128)S(1)} %stack.83), channel_id=1, replica_groups=mesh['dp'=16,'tensor'=2] {'dp','tensor'}, use_global_device_ids=true, to_apply=%region_47.48 | all-reduce | flops 14 | bytes 112 | tf_op jit(solution)/shard_map/psum | solution.py:282
  (438 shorter events, 346.6 us)
Async XLA Ops:
  7.2 122.9 %all-gather.10.cloned.1.call-start = ((), (), s32[]{:S(2)}) async-start(), calls=%async_computation.5 | async-start | bytes 1216512 | tf_op jit(solution)/shard_map/all_gather | solution.py:160
  8.8 144.1 %all-gather.8.cloned.1.call-start = ((), (), s32[]{:S(2)}) async-start(), calls=%async_computation.4 | async-start | bytes 3649536 | tf_op jit(solution)/shard_map/all_gather | solution.py:159
  9.9 2.2 collective-permute-start
  12.0 247.3 %all-gather.18.cloned.1.call-start = ((), (), s32[]{:S(2)}) async-start(), calls=%async_computation.10 | async-start | bytes 1622016 | tf_op jit(solution)/shard_map/all_gather | solution.py:161
  12.7 7.1 collective-permute-start.1
  16.8 257.7 %all-gather.14.cloned.1.call-start = ((), (), s32[]{:S(2)}) async-start(), calls=%async_computation.7 | async-start | bytes 2506752 | tf_op jit(solution)/shard_map/all_gather | solution.py:166
  20.7 9.3 collective-permute-start.2
  23.2 262.5 %all-gather.12.cloned.1.call-start = ((), (), s32[]{:S(2)}) async-start(), calls=%async_computation.6 | async-start | bytes 3538944 | tf_op jit(solution)/shard_map/all_gather | solution.py:189
  30.7 15.8 %collective-permute-start.3 = (bf16[8,37632]{1,0:T(8,128)(2,1)S(1)}, bf16[8,37632]{1,0:T(8,128)(2,1)S(1)}, u32[]{:S(2)}, u32[]{:S(2)}) collective-permute-start(bf16[8,37632]{1,0:T(8,128)(2,1)S(1)} %pad_maximum_fusion.2), channel_id=1, source_target_pairs={{0,8},{1,9},{2,10},{3,11},{4,12},{5,13},{6,14},{7,15},{8,0},{9,1},... | collective-permute-start | bytes 1806344 | tf_op jit(solution)/shard_map/ppermute | solution.py:33
  48.0 85.4 %collective-permute-start.4 = (bf16[16,37632]{1,0:T(8,128)(2,1)}, bf16[16,37632]{1,0:T(8,128)(2,1)S(1)}, u32[]{:S(2)}, u32[]{:S(2)}) collective-permute-start(bf16[16,37632]{1,0:T(8,128)(2,1)} %pad_maximum_fusion.1), channel_id=1, source_target_pairs={{0,16},{1,17},{2,18},{3,19},{4,20},{5,21},{6,22},{7,23},{8,24},{9,... | collective-permute-start | bytes 3612680 | tf_op jit(solution)/shard_map/ppermute | solution.py:33
  256.4 56.2 %all-gather.20.cloned.1.call-start = ((), (), s32[]{:S(2)}) async-start(), calls=%async_computation.11 | async-start | bytes 3538944 | tf_op jit(solution)/shard_map/all_gather | solution.py:210
  268.2 192.5 %reduce-scatter.11.cloned.1.call-start = ((), (), s32[]{:S(2)}) async-start(), calls=%async_computation.14 | async-start | bytes 5013504 | tf_op jit(solution)/shard_map/reduce_scatter | solution.py:224
  321.9 204.1 %all-gather.16.cloned.1.call-start = ((), (), s32[]{:S(2)}) async-start(), calls=%async_computation.8 | async-start | bytes 2506752 | tf_op jit(solution)/shard_map/all_gather | solution.py:167
  463.3 103.1 %reduce-scatter.5.cloned.1.call-start = ((), (), s32[]{:S(2)}) async-start(), calls=%async_computation.9 | async-start | bytes 3538944 | tf_op jit(solution)/shard_map/reduce_scatter | solution.py:192
  534.4 39.2 %reduce-scatter.7.cloned.1.call-start = ((), (), s32[]{:S(2)}) async-start(), calls=%async_computation.12 | async-start | bytes 7077888 | tf_op jit(solution)/shard_map/reduce_scatter | solution.py:216
  556.4 241.2 %reduce-scatter.9.cloned.1.call-start = ((), (), s32[]{:S(2)}) async-start(), calls=%async_computation.13 | async-start | bytes 5013504 | tf_op jit(solution)/shard_map/reduce_scatter | solution.py:223
  566.3 473.4 %all-reduce.10.cloned.1.call-start = ((), (), s32[]{:S(2)}) async-start(), calls=%async_computation.15 | async-start | bytes 34799616
  754.6 290.2 %copy-start.30 = (f32[24576]{0:T(1024)S(1)}, f32[24576]{0:T(1024)}, u32[]{:S(2)}) copy-start(f32[24576]{0:T(1024)} %param.43) | copy-start | bytes 294916
  754.6 290.2 %copy-start.38 = (f32[24576]{0:T(1024)S(1)}, f32[24576]{0:T(1024)}, u32[]{:S(2)}) copy-start(f32[24576]{0:T(1024)} %param.45) | copy-start | bytes 294916
  754.7 292.4 %copy-start.31 = (f32[18432]{0:T(1024)S(1)}, f32[18432]{0:T(1024)}, u32[]{:S(2)}) copy-start(f32[18432]{0:T(1024)} %param.40) | copy-start | bytes 221188
  754.7 292.4 %copy-start.40 = (f32[18432]{0:T(1024)S(1)}, f32[18432]{0:T(1024)}, u32[]{:S(2)}) copy-start(f32[18432]{0:T(1024)} %param.42) | copy-start | bytes 221188
  754.7 292.4 %copy-start.41 = (f32[18432]{0:T(1024)S(1)}, f32[18432]{0:T(1024)}, u32[]{:S(2)}) copy-start(f32[18432]{0:T(1024)} %param.41) | copy-start | bytes 221188
  799.9 312.8 %copy-start.28 = (f32[96,768]{1,0:T(8,128)}, f32[96,768]{1,0:T(8,128)S(1)}, u32[]{:S(2)}) copy-start(f32[96,768]{1,0:T(8,128)S(1)} %get-tuple-element.378) | copy-start | bytes 884740
  799.9 312.8 %copy-start.29 = (f32[96,768]{1,0:T(8,128)}, f32[96,768]{1,0:T(8,128)S(1)}, u32[]{:S(2)}) copy-start(f32[96,768]{1,0:T(8,128)S(1)} %get-tuple-element.379) | copy-start | bytes 884740
  (64 other events, 2837.0 us)
Sparse Core Ops, SparseCore 0:
  11.5 75.5 all-gather.9
  90.6 62.2 all-gather.7
  156.3 53.7 all-gather.17
  213.3 61.1 all-gather.13
  275.9 9.7 all-gather.11
  287.1 12.1 all-gather.19
  322.0 138.6 reduce-scatter.10
  464.4 61.4 all-gather.15
  534.6 8.7 reduce-scatter.4
  556.5 11.3 reduce-scatter.6
  574.0 138.6 reduce-scatter.8
  750.4 289.2 all-reduce.9
